TPU v7x, 32 devices: a whole 2x2x4 slice. The times are simulated.
32 devices in a mesh: rep: 2 (over y), head: 4 (over x, core), row: 4 (over z).
Axes of the slice: x: 2, y: 2, z: 4, core: 2. Of those that a mesh axis runs over, the one named last changes fastest.
Arguments:
- hidden: bfloat16 [256, 2, 8192], P(('rep', 'row'), None, 'head'), parts along dimension 0, may hold values from -6 to 6
- input_norm_scale: float32 [8192], P('head'), may hold values from 0.5 to 1.5
- projection_signal: bfloat16 [8192, 4096], P('row', 'head'), may hold values from -0.0625 to 0.0625
- projection_gate: bfloat16 [8192, 4096], P('row', 'head'), may hold values from -0.0625 to 0.0625
- projection_step: bfloat16 [8192, 64], P('row', 'head'), may hold values from -0.0625 to 0.0625
- projection_input_output: bfloat16 [8192, 256], P('row'), may hold values from -0.0625 to 0.0625
- step_bias: float32 [64], P('head'), may hold values from -4 to 0
- head_decay_rate: float32 [64], P('head'), may hold values from 0.5 to 16
- head_skip_weight: float32 [64], P('head'), may hold values from 0.5 to 1.5
- gated_norm_scale: float32 [4096], P('head'), may hold values from 0.5 to 1.5
- adapter_down_weight: bfloat16 [512, 8192, 16], P('row', 'head'), may hold values from -0.0625 to 0.0625
- adapter_up_weight: bfloat16 [512, 16, 4096], P('row', None, 'head'), may hold values from -1.5 to 1.5
- output_weight: bfloat16 [4096, 8192], P('head'), may hold values from -0.125 to 0.125
- scan_state: bfloat16 [256, 64, 64, 128], P(('rep', 'row'), 'head'), parts along dimension 0, may hold values from -6 to 6
- stream_tenant_index: int32 [256], P(('rep', 'row')), parts along dimension 0, may hold values from 0 to 511, as said below
- live_block_rows: int32 [8], P(('rep', 'row')), parts along dimension 0, may hold values from 1 to 32
Outputs:
- mixed: bfloat16 [256, 2, 8192], P(('rep', 'row'), None, 'head'), parts along dimension 0
- new_state: bfloat16 [256, 64, 64, 128], P(('rep', 'row'), 'head'), parts along dimension 0
There are 2 independent parts, one for each index of `rep`. A program takes and returns all parts, laid end to end along the dimension named above; an argument that names none is the same for every part. Nothing has to cross between parts.
Inputs may be any that keep to these rules, and one draw needn't show every extreme that they name: `stream_tenant_index`: a stream of block b has a tenant of b * 128 up to (b + 1) * 128 - 1.
All inputs are finite; a program needn't handle non-finite values.
Results may differ from a plain program's by a relative error of at most 0.02.
Values may be sent and summed in bfloat16 or wider, within the bound.
A program may use at most 128 MiB of HBM per device.

v0:
```python
import jax
import jax.numpy as jnp
from jax import lax
from jax.sharding import PartitionSpec as P

MODEL_WIDTH = 8192
INNER_WIDTH = 4096


def on_device(
    hidden,
    input_norm_scale,
    projection_signal,
    projection_gate,
    projection_step,
    projection_input_output,
    step_bias,
    head_decay_rate,
    head_skip_weight,
    gated_norm_scale,
    adapter_down_weight,
    adapter_up_weight,
    output_weight,
    scan_state,
    stream_tenant_index,
    live_block_rows,
):
    epsilon = 1e-05
    streams = hidden.shape[0]
    positions = hidden.shape[1]
    inner = projection_signal.shape[1]
    heads_here = projection_step.shape[1]
    state_width = projection_input_output.shape[1] // 2
    feature_width = hidden.shape[2]
    wide = hidden.astype(jnp.float32)
    tenant_local = stream_tenant_index - lax.axis_index("row") * adapter_down_weight.shape[0]
    scaled = (wide * input_norm_scale).astype(jnp.bfloat16)
    down_weight_rows = jnp.take(adapter_down_weight, tenant_local, axis=0)
    square_part = jnp.sum(wide * wide, -1)
    lowrank_part = jnp.einsum(
        "spd,sdr->spr", scaled, down_weight_rows, preferred_element_type=jnp.float32
    )
    squares, lowrank_sum = lax.psum((square_part, lowrank_part), "head")
    inverse = lax.rsqrt(squares / MODEL_WIDTH + epsilon)
    lowrank = (lowrank_sum * inverse[..., None]).astype(jnp.bfloat16)
    normed = (wide * input_norm_scale * inverse[..., None]).astype(jnp.bfloat16)
    features = lax.all_gather(normed, "head", axis=2, tiled=True)
    weight_cat = jnp.concatenate(
        [projection_signal, projection_gate, projection_step, projection_input_output], axis=1
    )
    moved = lax.all_to_all(features, "row", split_axis=2, concat_axis=0, tiled=True)
    moved_flat = moved.reshape(-1, moved.shape[2])
    projected = lax.psum_scatter(
        jnp.dot(moved_flat, weight_cat, preferred_element_type=jnp.float32).astype(jnp.bfloat16),
        "row",
        scatter_dimension=0,
        tiled=True,
    ).astype(jnp.float32)
    projected = projected.reshape(streams, positions, -1)
    xin = projected[..., :inner]
    zin = projected[..., inner : 2 * inner]
    dtin = projected[..., 2 * inner : 2 * inner + heads_here]
    bcin = projected[..., 2 * inner + heads_here :]
    up_weight_rows = jnp.take(adapter_up_weight, tenant_local, axis=0)
    signal = jax.nn.silu(
        xin
        + jnp.einsum("spr,srk->spk", lowrank, up_weight_rows, preferred_element_type=jnp.float32)
    )
    bgate = jax.nn.silu(bcin[..., :state_width])
    cgate = jax.nn.silu(bcin[..., state_width:])
    steps_dt = jax.nn.softplus(dtin + step_bias)
    decay = jnp.exp(-steps_dt * head_decay_rate)
    live = jnp.arange(streams) < live_block_rows[0]
    signal_heads = signal.reshape(streams, positions, heads_here, -1)
    carried = scan_state.astype(jnp.float32)
    outputs = []
    for position in range(positions):
        updated = (
            carried * decay[:, position, :, None, None]
            + (steps_dt[:, position, :, None] * signal_heads[:, position])[..., None]
            * bgate[:, position, None, None, :]
        )
        carried = jnp.where(live[:, None, None, None], updated, carried)
        outputs.append(
            jnp.sum(carried * cgate[:, position, None, None, :], -1)
            + head_skip_weight[None, :, None] * signal_heads[:, position]
        )
    new_state = carried.astype(jnp.bfloat16)
    result = jnp.stack(outputs, 1).reshape(streams, positions, inner)
    gated = result * jax.nn.silu(zin)
    gate_squares = lax.psum(jnp.sum(gated * gated, -1), "head")
    outnorm = (
        gated * lax.rsqrt(gate_squares / INNER_WIDTH + epsilon)[..., None] * gated_norm_scale
    ).astype(jnp.bfloat16)
    out_flat = outnorm.reshape(streams * positions, inner)
    partial_out = jnp.dot(out_flat, output_weight, preferred_element_type=jnp.float32)
    mixer = lax.psum_scatter(
        partial_out.astype(jnp.bfloat16), "head", scatter_dimension=1, tiled=True
    ).astype(jnp.float32)
    mixer = mixer.reshape(streams, positions, feature_width)
    mixed = (wide + jnp.where(live[:, None, None], mixer, 0.0)).astype(jnp.bfloat16)
    return (mixed, new_state)


def solution(mesh):
    in_specs = (
        P(("rep", "row"), None, "head"),
        P("head"),
        P("row", "head"),
        P("row", "head"),
        P("row", "head"),
        P("row", None),
        P("head"),
        P("head"),
        P("head"),
        P("head"),
        P("row", "head", None),
        P("row", None, "head"),
        P("head", None),
        P(("rep", "row"), "head", None, None),
        P(("rep", "row")),
        P(("rep", "row")),
    )
    out_specs = (P(("rep", "row"), None, "head"), P(("rep", "row"), "head", None, None))
    return jax.shard_map(
        on_device, mesh=mesh, in_specs=in_specs, out_specs=out_specs, check_vma=False
    )
```

profile of v0, /device:TPU:0, one launch (start us, length us, event | category | flops | bytes accessed | tf_op | source)
XLA Modules:
  0.0 219.4 jit_solution(15513517323388367327)
XLA Ops:
  7.2 0.0 all-gather.2.cloned.1.call-start
  7.2 0.7 compare_and_fusion
  7.9 0.0 copy-start
  7.9 0.0 copy-start.3
  7.9 4.1 %gather_fusion = bf16[32,2048,16]{1,2,0:T(8,128)(2,1)S(1)} fusion(bf16[128,2048,16]{1,2,0:T(8,128)(2,1)} %param.26, s32[1024]{0:T(1024)S(1)} %pad_clamp_fusion), kind=kCustom, calls=%fused_computation | custom fusion | bytes 4194432 | tf_op jit(solution)/shard_map/jit(_take)/gather | solution.py:38
  12.0 0.0 copy-done
  12.0 0.0 copy-done.3
  12.0 0.0 copy-start.2
  12.1 0.0 copy-start.1
  12.1 0.2 fusion.8
  12.2 1.0 fusion.2
  13.3 13.8 %all-reduce = (f32[32,2]{0,1:T(2,128)S(1)}, f32[32,2,16]{2,1,0:T(2,128)}) all-reduce(f32[32,2]{0,1:T(2,128)S(1)} %get-tuple-element.32, f32[32,2,16]{2,1,0:T(2,128)S(1)} %fusion.2), channel_id=1, replica_groups=mesh['rep'=2,'head'=4,'row'=4] {'head'}, use_global_device_ids=true, to_apply=%region_1.2 | all-reduce | flops 1088 | bytes 8704 | tf_op jit(solution)/shard_map/psum | solution.py:43
  27.0 0.8 fusion.10
  27.8 0.0 all-gather.2.cloned.1.call-update
  27.9 17.2 %all-gather.2.cloned.1.call-done = bf16[32,2,8192]{2,0,1:T(8,128)(2,1)} async-done(((bf16[32,2,2048]{2,0,1:T(8,128)(2,1)}), bf16[32,2,8192]{2,0,1:T(8,128)(2,1)}) %all-gather.2.cloned.1.call-update) | async-done | bytes 1048592 | tf_op jit(solution)/shard_map/all_gather | solution.py:47
  45.0 9.2 %copy.76 = bf16[32,2,8192]{0,1,2:T(2,128)(2,1)} copy(bf16[32,2,8192]{2,0,1:T(8,128)(2,1)} %all-gather.2.cloned.1.call-done) | data formatting | bytes 2097152 | tf_op jit(solution)/shard_map/all_gather | solution.py:47
  54.2 6.4 %reshape.98 = bf16[4,2,65536]{2,1,0:T(2,128)(2,1)} reshape(bf16[8192,2,32]{2,1,0:T(2,128)(2,1)} %bitcast.34) | data formatting | bytes 2097152
  60.6 4.6 %all-to-all-start = ((bf16[4,2,65536]{2,1,0:T(2,128)(2,1)}), bf16[4,2,65536]{2,1,0:T(2,128)(2,1)S(1)}, u32[]{:S(2)}, u32[]{:S(2)}) async-start(bf16[4,2,65536]{2,1,0:T(2,128)(2,1)} %reshape.98), calls=%async_computation | async-start | bytes 2097152 | tf_op jit(solution)/shard_map/all_to_all | solution.py:51
  65.2 0.0 reduce-scatter.3.cloned.1.call-start
  65.2 0.3 copy.78
  65.5 15.0 %concatenate.4 = bf16[2048,2320]{1,0:T(8,128)(2,1)} concatenate(bf16[2048,1024]{1,0:T(8,128)(2,1)} %param.18, bf16[2048,1024]{1,0:T(8,128)(2,1)} %param.19, bf16[2048,16]{1,0:T(8,128)(2,1)S(1)} %copy.78, bf16[2048,256]{1,0:T(8,128)(2,1)S(1)} %copy-done.1), dimensions={1} | concatenate | bytes 19005440 | tf_op jit(solution)/shard_map/concatenate | solution.py:48
  80.5 10.8 %all-to-all-done = bf16[4,2,65536]{2,1,0:T(2,128)(2,1)S(1)} async-done(((bf16[4,2,65536]{2,1,0:T(2,128)(2,1)}), bf16[4,2,65536]{2,1,0:T(2,128)(2,1)S(1)}, u32[]{:S(2)}, u32[]{:S(2)}) %all-to-all-start) | async-done | bytes 1048608 | tf_op jit(solution)/shard_map/all_to_all | solution.py:51
  91.3 3.5 %reshape.99 = bf16[8192,2,32]{2,1,0:T(2,128)(2,1)} reshape(bf16[4,2,65536]{2,1,0:T(2,128)(2,1)S(1)} %all-to-all-done) | data formatting | bytes 2097152
  94.7 9.7 %copy.77 = bf16[32,2,4,2048]{3,1,0,2:T(2,128)(2,1)S(1)} copy(bf16[32,2,4,2048]{0,1,3,2:T(2,128)(2,1)} %bitcast.35) | data formatting | bytes 2097152 | tf_op jit(solution)/shard_map/all_to_all | solution.py:51
  104.4 0.4 reshape.69
  104.9 7.7 %convolution_convert_fusion.1 = bf16[256,2320]{1,0:T(8,128)(2,1)} fusion(bf16[256,2048]{1,0:T(8,128)(2,1)S(1)} %reshape.69, bf16[2048,2320]{1,0:T(8,128)(2,1)} %concatenate.4), kind=kOutput, calls=%fused_computation.10 | convolution fusion | flops 2433290240 | bytes 11739136 | tf_op jit(solution)/shard_map/dot_general | solution.py:54
  112.7 0.0 reduce-scatter.3.cloned.1.call-update
  112.7 0.0 reduce-scatter.5.cloned.1.call-start
  112.7 0.1 copy.83
  112.8 2.8 %gather_fusion.1 = bf16[32,16,1024]{2,1,0:T(8,128)(2,1)S(1)} fusion(bf16[128,16,1024]{2,1,0:T(8,128)(2,1)} %param.27, s32[1024]{0:T(1024)S(1)} %pad_clamp_fusion), kind=kCustom, calls=%fused_computation.1 | custom fusion | bytes 2097280 | tf_op jit(solution)/shard_map/jit(_take)/gather | solution.py:64
  116.3 25.0 %reduce-scatter.3.cloned.1.call-done = bf16[64,2320]{1,0:T(8,128)(2,1)} async-done(((bf16[256,2320]{1,0:T(8,128)(2,1)}), bf16[64,2320]{1,0:T(8,128)(2,1)}) %reduce-scatter.3.cloned.1.call-update) | async-done | bytes 296976 | tf_op jit(solution)/shard_map/reduce_scatter | solution.py:53
  141.3 1.3 reshape.77
  142.6 0.1 divide_multiply_fusion.3
  142.8 0.5 divide_multiply_fusion.1
  143.3 0.0 copy-start.7
  143.3 0.3 reshape.72
  143.6 0.1 copy.90
  143.7 0.0 copy-done.5
  143.7 0.1 multiply_exponential_fusion
  143.8 0.1 copy.81
  143.9 0.1 copy.85
  144.0 0.1 copy.80
  144.0 0.1 copy.84
  144.1 0.1 fusion.22
  144.2 0.2 bitcast_multiply_fusion
  144.4 0.0 copy-start.4
  144.4 24.9 %multiply_reduce_fusion.1 = (f32[32,16,64]{2,1,0:T(8,128)S(1)}, f32[32,16,64]{2,1,0:T(8,128)S(1)}, bf16[32,16,64,128]{3,2,1,0:T(8,128)(2,1)}) fusion(bf16[32,16,64,128]{3,2,1,0:T(8,128)(2,1)} %param.29, f32[32,128]{1,0:T(8,128)S(1)} %bitcast.39, f32[32,128]{1,0:T(8,128)S(1)} %bitcast.38, f32[32,16,64]{2,1,0:T(8,128)S(1)} %get-tuple-element.30, ...), kind=kLoop, calls=%fused_computation.7 | loop fusion | flops 58654720 | bytes 17371168 | tf_op jit(solution)/shard_map/reduce_sum | solution.py:85
  169.3 0.0 copy-done.7
  169.3 0.1 bitcast_add_fusion.1
  169.4 0.2 stack.10
  169.6 0.2 stack.9
  169.8 0.6 multiply_reduce_fusion.2
  170.4 0.1 copy.86
  170.4 6.3 %psum.23 = f32[32,2]{0,1:T(2,128)S(1)} all-reduce(f32[32,2]{0,1:T(2,128)S(1)} %copy.86), channel_id=1, replica_groups=mesh['rep'=2,'head'=4,'row'=4] {'head'}, use_global_device_ids=true, to_apply=%region_7.8 | all-reduce | flops 64 | bytes 512 | tf_op jit(solution)/shard_map/psum | solution.py:91
  176.8 0.1 copy.87
  176.9 0.0 copy-done.4
  176.9 0.2 multiply_convert_fusion
  177.1 0.1 reshape.73
  177.1 9.8 %convolution_convert_fusion = bf16[64,8192]{1,0:T(8,128)(2,1)} fusion(bf16[64,1024]{1,0:T(8,128)(2,1)S(1)} %reshape.73, bf16[1024,8192]{1,0:T(8,128)(2,1)} %param.28), kind=kOutput, calls=%fused_computation.9 | convolution fusion | flops 1074266112 | bytes 17956864 | tf_op jit(solution)/shard_map/dot_general | solution.py:96
  186.9 0.0 reduce-scatter.5.cloned.1.call-update
  186.9 23.3 %reduce-scatter.5.cloned.1.call-done = bf16[64,2048]{1,0:T(8,128)(2,1)} async-done(((bf16[64,8192]{1,0:T(8,128)(2,1)}), bf16[64,2048]{1,0:T(8,128)(2,1)}) %reduce-scatter.5.cloned.1.call-update) | async-done | bytes 262160 | tf_op jit(solution)/shard_map/reduce_scatter | solution.py:97
  210.3 1.3 reshape.79
  211.5 0.4 fusion.12
  211.9 1.0 copy.89
  (13 shorter events, 0.1 us)
Async XLA Ops:
  7.2 37.9 %all-gather.2.cloned.1.call-start = ((), (), s32[]{:S(2)}) async-start(), calls=%async_computation.3 | async-start | bytes 1310720 | tf_op jit(solution)/shard_map/all_gather | solution.py:47
  7.9 4.1 %copy-start = (bf16[32,2,2048]{2,1,0:T(2,128)(2,1)S(1)}, bf16[32,2,2048]{2,1,0:T(2,128)(2,1)}, u32[]{:S(2)}) copy-start(bf16[32,2,2048]{2,1,0:T(2,128)(2,1)} %param.16) | copy-start | bytes 786436
  7.9 4.1 %copy-start.3 = (f32[2048]{0:T(1024)S(1)}, f32[2048]{0:T(1024)}, u32[]{:S(2)}) copy-start(f32[2048]{0:T(1024)} %param.17) | copy-start | bytes 24580
  12.0 53.1 %copy-start.2 = (bf16[2048,16]{0,1:T(8,128)(2,1)S(1)}, bf16[2048,16]{0,1:T(8,128)(2,1)}, u32[]{:S(2)}) copy-start(bf16[2048,16]{0,1:T(8,128)(2,1)} %param.20) | copy-start | bytes 196612
  12.1 53.4 %copy-start.1 = (bf16[2048,256]{1,0:T(8,128)(2,1)S(1)}, bf16[2048,256]{1,0:T(8,128)(2,1)}, u32[]{:S(2)}) copy-start(bf16[2048,256]{1,0:T(8,128)(2,1)} %param.21) | copy-start | bytes 3145732
  60.6 30.7 %all-to-all-start = ((bf16[4,2,65536]{2,1,0:T(2,128)(2,1)}), bf16[4,2,65536]{2,1,0:T(2,128)(2,1)S(1)}, u32[]{:S(2)}, u32[]{:S(2)}) async-start(bf16[4,2,65536]{2,1,0:T(2,128)(2,1)} %reshape.98), calls=%async_computation | async-start | bytes 2097152 | tf_op jit(solution)/shard_map/all_to_all | solution.py:51
  65.2 76.1 %reduce-scatter.3.cloned.1.call-start = ((), (), s32[]{:S(2)}) async-start(), calls=%async_computation.4 | async-start | bytes 1556480 | tf_op jit(solution)/shard_map/reduce_scatter | solution.py:53
  104.9 37.9 %copy-start.8 = (f32[32,2,16]{2,1,0:T(2,128)S(1)}, f32[32,2,16]{2,1,0:T(2,128)}, u32[]{:S(2)}) copy-start(f32[32,2,16]{2,1,0:T(2,128)} %get-tuple-element.17) | copy-start | bytes 12292
  112.6 31.0 %copy-start.5 = (f32[16]{0:T(128)S(1)}, f32[16]{0:T(128)}, u32[]{:S(2)}) copy-start(f32[16]{0:T(128)} %param.23) | copy-start | bytes 196
  112.6 31.0 %copy-start.6 = (f32[16]{0:T(128)S(1)}, f32[16]{0:T(128)}, u32[]{:S(2)}) copy-start(f32[16]{0:T(128)} %param.22) | copy-start | bytes 196
  112.7 97.6 %reduce-scatter.5.cloned.1.call-start = ((), (), s32[]{:S(2)}) async-start(), calls=%async_computation.5 | async-start | bytes 1310720 | tf_op jit(solution)/shard_map/reduce_scatter | solution.py:97
  143.3 26.0 %copy-start.7 = (f32[16]{0:T(128)S(1)}, f32[16]{0:T(128)}, u32[]{:S(2)}) copy-start(f32[16]{0:T(128)} %param.24) | copy-start | bytes 196
  144.4 32.5 %copy-start.4 = (f32[1024]{0:T(1024)S(1)}, f32[1024]{0:T(1024)}, u32[]{:S(2)}) copy-start(f32[1024]{0:T(1024)} %param.25) | copy-start | bytes 12292
Sparse Core Ops, SparseCore 0:
  28.0 17.0 all-gather.1
  112.8 28.4 reduce-scatter.2
  187.0 23.1 reduce-scatter.4
where the time goes:
time: 221 us; the launch traced here: 219 us
  waiting for transfers between devices  76.4 us (35%)
  local copies, waits for them, and re-layouts  56.3 us (25%)
  other arithmetic  28.3 us (13%)
  blocking collectives  20.1 us (9%)
  matrix products  19 us (9%)
  between operations  14.6 us (7%)
  starting transfers between devices  4.68 us (2%)
    reduce_scatter x1, waiting for transfers between devices, on_device(): lax.psum_scatter(jnp.dot(moved_flat, weight_cat, preferred_element_type=j...  25 us
    reduce_sum x1, other arithmetic, on_device(): jnp.sum(carried * cgate[:, position, None, None, :], -1)  24.9 us
    reduce_scatter x1, waiting for transfers between devices, on_device(): lax.psum_scatter(partial_out.astype(jnp.bfloat16), 'head', scatter_dimens...  23.3 us
    all_gather x1, waiting for transfers between devices, on_device(): features = lax.all_gather(normed, 'head', axis=2, tiled=True)  17.2 us
    concatenate x1, local copies, waits for them, and re-layouts, on_device(): jnp.concatenate([projection_signal, projection_gate, projection_step, pro...  15 us
    psum x1, blocking collectives, on_device(): squares, lowrank_sum = lax.psum((square_part, lowrank_part), 'head')  13.8 us
    unnamed x23, local copies, waits for them, and re-layouts  11.2 us
    all_to_all x1, waiting for transfers between devices, on_device(): lax.all_to_all(features, 'row', split_axis=2, concat_axis=0, tiled=True)  10.8 us
  transfers between devices with their start and end apart: 4, of which 4 were waited for; matrix products, arithmetic and copies ran while one was open for 8% of the time, Pallas kernels for 0%

commit v1 on v0

--- a/solution.py
+++ b/solution.py
@@ -48,7 +48,10 @@
     weight_cat = jnp.concatenate(
         [projection_signal, projection_gate, projection_step, projection_input_output], axis=1
     )
-    moved = lax.all_to_all(features, "row", split_axis=2, concat_axis=0, tiled=True)
+    moved = jnp.concatenate(
+        lax.all_to_all(jnp.stack(jnp.split(features, lax.axis_size("row"), axis=2)), "row", 0, 0),
+        axis=0,
+    )
     moved_flat = moved.reshape(-1, moved.shape[2])
     projected = lax.psum_scatter(
         jnp.dot(moved_flat, weight_cat, preferred_element_type=jnp.float32).astype(jnp.bfloat16),

time: 221 us -> 202 us (0.914)
  local copies, waits for them, and re-layouts: 56.3 us -> 28.6 us
  other arithmetic: 28.3 us -> 33 us
  blocking collectives: 20.1 us -> 24.3 us
    unnamed x23 -> x20, local copies, waits for them, and re-layouts: 11.2 us -> 0.39 us
    all_to_all x1 -> x0, local copies, waits for them, and re-layouts: 9.69 us -> none  [on_device(): lax.all_to_all(features, 'row', split_axis=2, concat_axis=0, tiled=True)]
    all_gather x1 -> x0, local copies, waits for them, and re-layouts: 9.15 us -> none  [on_device(): features = lax.all_gather(normed, 'head', axis=2, tiled=True)]
    psum x1, blocking collectives: 6.33 us -> 10.5 us  [on_device(): gate_squares = lax.psum(jnp.sum(gated * gated, -1), 'head')]
    another operation x0 -> x1, other arithmetic: none -> 2.74 us  [on_device(): jnp.stack(jnp.split(features, lax.axis_size('row'), axis=2))]
    another operation x0 -> x2, local copies, waits for them, and re-layouts: none -> 2.62 us  [the longest x1 2.2 us: on_device(): jnp.stack(jnp.split(features, lax.axis_size('row'), axis=2))]
  transfers between devices with their start and end apart: 4 -> 4, of which waited for: 4 -> 4; matrix products, arithmetic and copies ran while one was open for 8% -> 9% of each run, Pallas kernels for 0% -> 0%
where the time goes in v1:
time: 202 us; the launch traced here: 201 us
  waiting for transfers between devices  76.5 us (38%)
  other arithmetic  33 us (16%)
  local copies, waits for them, and re-layouts  28.6 us (14%)
  blocking collectives  24.3 us (12%)
  matrix products  19 us (9%)
  between operations  14.6 us (7%)
  starting transfers between devices  4.68 us (2%)
    reduce_scatter x1, waiting for transfers between devices, on_device(): lax.psum_scatter(jnp.dot(moved_flat, weight_cat, preferred_element_type=j...  25.1 us
    reduce_sum x1, other arithmetic, on_device(): jnp.sum(carried * cgate[:, position, None, None, :], -1)  24.9 us
    reduce_scatter x1, waiting for transfers between devices, on_device(): lax.psum_scatter(partial_out.astype(jnp.bfloat16), 'head', scatter_dimens...  23.4 us
    all_gather x1, waiting for transfers between devices, on_device(): features = lax.all_gather(normed, 'head', axis=2, tiled=True)  17.2 us
    concatenate x1, local copies, waits for them, and re-layouts, on_device(): jnp.concatenate([projection_signal, projection_gate, projection_step, pro...  15 us
    psum x1, blocking collectives, on_device(): squares, lowrank_sum = lax.psum((square_part, lowrank_part), 'head')  13.8 us
    all_to_all x1, waiting for transfers between devices, on_device(): lax.all_to_all(jnp.stack(jnp.split(features, lax.axis_size('row'), axis=2...  10.8 us
    psum x1, blocking collectives, on_device(): gate_squares = lax.psum(jnp.sum(gated * gated, -1), 'head')  10.5 us
  transfers between devices with their start and end apart: 4, of which 4 were waited for; matrix products, arithmetic and copies ran while one was open for 9% of the time, Pallas kernels for 0%

profile of v1, /device:TPU:0, one launch (start us, length us, event | category | flops | bytes accessed | tf_op | source)
XLA Modules:
  0.0 200.8 jit_solution(208756091860985009)
XLA Ops:
  7.2 0.0 all-gather.2.cloned.1.call-start
  7.2 0.7 compare_and_fusion
  7.9 1.3 fusion.11
  9.2 0.0 copy-start
  9.2 4.1 %gather_fusion = bf16[32,2048,16]{1,2,0:T(8,128)(2,1)S(1)} fusion(bf16[128,2048,16]{1,2,0:T(8,128)(2,1)} %param.26, s32[1024]{0:T(1024)S(1)} %pad_clamp_fusion), kind=kCustom, calls=%fused_computation | custom fusion | bytes 4194432 | tf_op jit(solution)/shard_map/jit(_take)/gather | solution.py:38
  13.3 0.0 copy-start.2
  13.3 0.0 copy-start.1
  13.3 0.0 copy-done
  13.3 0.0 copy-done.3
  13.4 1.0 fusion.2
  14.4 13.8 %all-reduce = (f32[32,2]{1,0:T(8,128)S(1)}, f32[32,2,16]{2,1,0:T(2,128)}) all-reduce(f32[32,2]{1,0:T(8,128)S(1)} %fusion.11, f32[32,2,16]{2,1,0:T(2,128)S(1)} %fusion.2), channel_id=1, replica_groups=mesh['rep'=2,'head'=4,'row'=4] {'head'}, use_global_device_ids=true, to_apply=%region_1.2 | all-reduce | flops 1088 | bytes 8704 | tf_op jit(solution)/shard_map/psum | solution.py:43
  28.2 1.0 fusion.10
  29.2 0.0 all-gather.2.cloned.1.call-update
  29.2 17.2 %all-gather.2.cloned.1.call-done = bf16[32,2,8192]{2,1,0:T(2,128)(2,1)} async-done(((bf16[32,2,2048]{2,1,0:T(2,128)(2,1)}), bf16[32,2,8192]{2,1,0:T(2,128)(2,1)}) %all-gather.2.cloned.1.call-update) | async-done | bytes 1048592 | tf_op jit(solution)/shard_map/all_gather | solution.py:47
  46.4 2.2 %slice_bitcast_fusion.3 = (bf16[1,32,2,2048]{3,2,1,0:T(2,128)(2,1)S(1)}, bf16[1,32,2,2048]{3,2,1,0:T(2,128)(2,1)S(1)}, bf16[1,32,2,2048]{3,2,1,0:T(2,128)(2,1)S(1)}, bf16[1,32,2,2048]{3,2,1,0:T(2,128)(2,1)S(1)}) fusion(bf16[32,2,8192]{2,1,0:T(2,128)(2,1)} %all-gather.2.cloned.1.call-done), kind=kLoop, calls=%fused_computation.34 | loop fusion | bytes 2097152 | tf_op jit(solution)/shard_map/stack | solution.py:52
  48.6 2.7 %pad_maximum_fusion = bf16[4,32,2,2048]{3,2,1,0:T(2,128)(2,1)} fusion(bf16[1,32,2,2048]{3,2,1,0:T(2,128)(2,1)S(1)} %get-tuple-element.14, bf16[1,32,2,2048]{3,2,1,0:T(2,128)(2,1)S(1)} %get-tuple-element.15, bf16[1,32,2,2048]{3,2,1,0:T(2,128)(2,1)S(1)} %get-tuple-element.16, bf16[1,32,2,2048]{3,2,1,0:T(2,128)(2,1)S(1)} %get-tuple-element.13), kind=kLoop, calls=%fused_computation.15 | loop fusion | flops 1572864 | bytes 2097152 | tf_op jit(solution)/shard_map/stack | solution.py:52
  51.4 4.6 %all-to-all-start = ((bf16[4,32,2,2048]{3,2,1,0:T(2,128)(2,1)}), bf16[4,32,2,2048]{3,2,1,0:T(2,128)(2,1)S(1)}, u32[]{:S(2)}, u32[]{:S(2)}) async-start(bf16[4,32,2,2048]{3,2,1,0:T(2,128)(2,1)} %pad_maximum_fusion), calls=%async_computation | async-start | bytes 2097152 | tf_op jit(solution)/shard_map/all_to_all | solution.py:52
  56.0 0.0 reduce-scatter.3.cloned.1.call-start
  56.0 0.0 copy-done.2
  56.0 0.3 copy.31
  56.2 0.0 copy-done.1
  56.2 15.0 %concatenate.4 = bf16[2048,2320]{1,0:T(8,128)(2,1)} concatenate(bf16[2048,1024]{1,0:T(8,128)(2,1)} %param.18, bf16[2048,1024]{1,0:T(8,128)(2,1)} %param.19, bf16[2048,16]{1,0:T(8,128)(2,1)S(1)} %copy.31, bf16[2048,256]{1,0:T(8,128)(2,1)S(1)} %copy-done.1), dimensions={1} | concatenate | bytes 19005440 | tf_op jit(solution)/shard_map/concatenate | solution.py:48
  71.2 10.8 %all-to-all-done = bf16[4,32,2,2048]{3,2,1,0:T(2,128)(2,1)S(1)} async-done(((bf16[4,32,2,2048]{3,2,1,0:T(2,128)(2,1)}), bf16[4,32,2,2048]{3,2,1,0:T(2,128)(2,1)S(1)}, u32[]{:S(2)}, u32[]{:S(2)}) %all-to-all-start) | async-done | bytes 1048608 | tf_op jit(solution)/shard_map/all_to_all | solution.py:52
  82.1 0.4 reshape_reshape.3
  82.5 0.0 copy-start.5
  82.5 0.0 copy-start.6
  82.5 0.0 copy-start.8
  82.5 7.8 %convolution_convert_fusion.1 = bf16[256,2320]{1,0:T(8,128)(2,1)} fusion(bf16[256,2048]{1,0:T(8,128)(2,1)S(1)} %reshape_reshape.3, bf16[2048,2320]{1,0:T(8,128)(2,1)} %concatenate.4), kind=kOutput, calls=%fused_computation.10 | convolution fusion | flops 2433290240 | bytes 11739136 | tf_op jit(solution)/shard_map/dot_general | solution.py:57
  90.3 0.0 reduce-scatter.3.cloned.1.call-update
  90.3 0.0 reduce-scatter.5.cloned.1.call-start
  90.4 2.8 %gather_fusion.1 = bf16[32,16,1024]{2,1,0:T(8,128)(2,1)S(1)} fusion(bf16[128,16,1024]{2,1,0:T(8,128)(2,1)} %param.27, s32[1024]{0:T(1024)S(1)} %pad_clamp_fusion), kind=kCustom, calls=%fused_computation.1 | custom fusion | bytes 2097280 | tf_op jit(solution)/shard_map/jit(_take)/gather | solution.py:67
  93.8 25.1 %reduce-scatter.3.cloned.1.call-done = bf16[64,2320]{1,0:T(8,128)(2,1)} async-done(((bf16[256,2320]{1,0:T(8,128)(2,1)}), bf16[64,2320]{1,0:T(8,128)(2,1)}) %reduce-scatter.3.cloned.1.call-update) | async-done | bytes 296976 | tf_op jit(solution)/shard_map/reduce_scatter | solution.py:56
  118.9 1.3 reshape.72
  120.2 0.1 divide_multiply_fusion.3
  120.4 0.1 copy.37
  120.5 0.0 copy-done.5
  120.5 0.0 copy-done.6
  120.5 0.1 multiply_exponential_fusion
  120.6 0.1 copy.34
  120.7 0.1 copy.36
  120.7 0.0 copy-done.8
  120.8 0.5 divide_multiply_fusion.1
  121.3 0.0 copy-start.7
  121.3 0.3 reshape.67
  121.6 0.1 copy.33
  121.7 0.1 copy.35
  121.7 0.1 fusion.23
  121.8 0.2 bitcast_multiply_fusion
  122.0 0.0 copy-start.4
  122.0 24.9 %multiply_reduce_fusion.1 = (f32[32,16,64]{2,1,0:T(8,128)S(1)}, f32[32,16,64]{2,1,0:T(8,128)S(1)}, bf16[32,16,64,128]{3,2,1,0:T(8,128)(2,1)}) fusion(bf16[32,16,64,128]{3,2,1,0:T(8,128)(2,1)} %param.29, f32[32,128]{1,0:T(8,128)S(1)} %bitcast.40, f32[32,128]{1,0:T(8,128)S(1)} %bitcast.39, f32[32,16,64]{2,1,0:T(8,128)S(1)} %get-tuple-element.22, ...), kind=kLoop, calls=%fused_computation.7 | loop fusion | flops 58654720 | bytes 17371168 | tf_op jit(solution)/shard_map/reduce_sum | solution.py:88
  146.9 0.0 copy-done.7
  146.9 0.1 bitcast_add_fusion.1
  147.0 0.2 stack.29
  147.2 0.2 stack.30
  147.4 0.6 multiply_reduce_fusion.2
  148.0 10.5 %psum.23 = f32[32,2]{1,0:T(8,128)S(1)} all-reduce(f32[32,2]{1,0:T(8,128)S(1)} %get-tuple-element.6), channel_id=1, replica_groups=mesh['rep'=2,'head'=4,'row'=4] {'head'}, use_global_device_ids=true, to_apply=%region_7.8 | all-reduce | flops 64 | bytes 512 | tf_op jit(solution)/shard_map/psum | solution.py:94
  158.5 0.0 copy-done.4
  158.5 0.2 multiply_convert_fusion
  158.7 0.1 reshape.68
  158.8 9.8 %convolution_convert_fusion = bf16[64,8192]{1,0:T(8,128)(2,1)} fusion(bf16[64,1024]{1,0:T(8,128)(2,1)S(1)} %reshape.68, bf16[1024,8192]{1,0:T(8,128)(2,1)} %param.28), kind=kOutput, calls=%fused_computation.9 | convolution fusion | flops 1074266112 | bytes 17956864 | tf_op jit(solution)/shard_map/dot_general | solution.py:99
  168.5 0.0 reduce-scatter.5.cloned.1.call-update
  168.6 23.4 %reduce-scatter.5.cloned.1.call-done = bf16[64,2048]{1,0:T(8,128)(2,1)} async-done(((bf16[64,8192]{1,0:T(8,128)(2,1)}), bf16[64,2048]{1,0:T(8,128)(2,1)}) %reduce-scatter.5.cloned.1.call-update) | async-done | bytes 262160 | tf_op jit(solution)/shard_map/reduce_scatter | solution.py:100
  191.9 1.3 reshape.74
  193.2 1.1 fusion.12
  (7 shorter events, 0.1 us)
Async XLA Ops:
  7.2 39.2 %all-gather.2.cloned.1.call-start = ((), (), s32[]{:S(2)}) async-start(), calls=%async_computation.3 | async-start | bytes 1310720 | tf_op jit(solution)/shard_map/all_gather | solution.py:47
  9.2 4.1 %copy-start = (bf16[32,2,2048]{2,1,0:T(2,128)(2,1)S(1)}, bf16[32,2,2048]{2,1,0:T(2,128)(2,1)}, u32[]{:S(2)}) copy-start(bf16[32,2,2048]{2,1,0:T(2,128)(2,1)} %param.16) | copy-start | bytes 786436
  9.2 4.2 %copy-start.3 = (f32[2048]{0:T(1024)S(1)}, f32[2048]{0:T(1024)}, u32[]{:S(2)}) copy-start(f32[2048]{0:T(1024)} %param.17) | copy-start | bytes 24580
  13.3 42.7 %copy-start.2 = (bf16[2048,16]{0,1:T(8,128)(2,1)S(1)}, bf16[2048,16]{0,1:T(8,128)(2,1)}, u32[]{:S(2)}) copy-start(bf16[2048,16]{0,1:T(8,128)(2,1)} %param.20) | copy-start | bytes 196612
  13.3 42.9 %copy-start.1 = (bf16[2048,256]{1,0:T(8,128)(2,1)S(1)}, bf16[2048,256]{1,0:T(8,128)(2,1)}, u32[]{:S(2)}) copy-start(bf16[2048,256]{1,0:T(8,128)(2,1)} %param.21) | copy-start | bytes 3145732
  51.4 30.7 %all-to-all-start = ((bf16[4,32,2,2048]{3,2,1,0:T(2,128)(2,1)}), bf16[4,32,2,2048]{3,2,1,0:T(2,128)(2,1)S(1)}, u32[]{:S(2)}, u32[]{:S(2)}) async-start(bf16[4,32,2,2048]{3,2,1,0:T(2,128)(2,1)} %pad_maximum_fusion), calls=%async_computation | async-start | bytes 2097152 | tf_op jit(solution)/shard_map/all_to_all | solution.py:52
  56.0 63.0 %reduce-scatter.3.cloned.1.call-start = ((), (), s32[]{:S(2)}) async-start(), calls=%async_computation.4 | async-start | bytes 1556480 | tf_op jit(solution)/shard_map/reduce_scatter | solution.py:56
  82.5 38.0 %copy-start.5 = (f32[16]{0:T(128)S(1)}, f32[16]{0:T(128)}, u32[]{:S(2)}) copy-start(f32[16]{0:T(128)} %param.23) | copy-start | bytes 196
  82.5 38.0 %copy-start.6 = (f32[16]{0:T(128)S(1)}, f32[16]{0:T(128)}, u32[]{:S(2)}) copy-start(f32[16]{0:T(128)} %param.22) | copy-start | bytes 196
  82.5 38.2 %copy-start.8 = (f32[32,2,16]{2,1,0:T(2,128)S(1)}, f32[32,2,16]{2,1,0:T(2,128)}, u32[]{:S(2)}) copy-start(f32[32,2,16]{2,1,0:T(2,128)} %get-tuple-element.5) | copy-start | bytes 12292
  90.3 101.6 %reduce-scatter.5.cloned.1.call-start = ((), (), s32[]{:S(2)}) async-start(), calls=%async_computation.5 | async-start | bytes 1310720 | tf_op jit(solution)/shard_map/reduce_scatter | solution.py:100
  121.3 25.6 %copy-start.7 = (f32[16]{0:T(128)S(1)}, f32[16]{0:T(128)}, u32[]{:S(2)}) copy-start(f32[16]{0:T(128)} %param.24) | copy-start | bytes 196
  122.0 36.5 %copy-start.4 = (f32[1024]{0:T(1024)S(1)}, f32[1024]{0:T(1024)}, u32[]{:S(2)}) copy-start(f32[1024]{0:T(1024)} %param.25) | copy-start | bytes 12292
Sparse Core Ops, SparseCore 0:
  29.4 17.0 all-gather.1
  90.4 28.4 reduce-scatter.2
  168.7 23.2 reduce-scatter.4
